TPU v7x, 512 devices: a whole 4x4x16 slice. The times are simulated.
512 devices in a mesh: wide: 64 (over x, y, z_hi), grp: 8 (over z_lo, core).
Axes of the slice: x: 4, y: 4, z: 16 (z_hi: 4, z_lo: 4; z = z_hi * 4 + z_lo), core: 2. Of those that a mesh axis runs over, the one named last changes fastest.
Arguments:
- samples: bfloat16 [2048, 512], P(('wide', 'grp')), may hold values from -6 to 6
- archive: bfloat16 [262144, 512], P(('wide', 'grp')), may hold values from -6 to 6
- inv_len: float32 [512], replicated, may hold values from 0.7 to 2.8
- mean_coef: bfloat16 [262144, 64], P(('wide', 'grp')), may hold values from -0.1875 to 0.1875
- var_coef: bfloat16 [262144, 64], P(('wide', 'grp')), may hold values from -1 to 1
Outputs:
- pred_mean: float32 [2048, 64], P(('wide', 'grp'))
- pred_var: float32 [2048, 64], P(('wide', 'grp'))
All inputs are finite; a program needn't handle non-finite values.
Results may differ from a plain program's by a relative error of at most 0.0085.
Values may be sent and summed in bfloat16 or wider, within the bound.
A program may use at most 64 MiB of HBM per device.

v0:
```python
import jax
import jax.numpy as jnp
from jax import lax
from jax.sharding import PartitionSpec as P

DIN = 512


def scaled_rows(rows, inv_len):
    factor = inv_len * DIN ** (-0.5)
    scaled = (rows.astype(jnp.float32) * factor).astype(jnp.bfloat16)
    wide_copy = scaled.astype(jnp.float32)
    return (scaled, jnp.sum(wide_copy * wide_copy, axis=-1))


def on_device(samples, archive, inv_len, mean_coef, var_coef):
    gathered = lax.all_gather(samples, ("wide", "grp"), axis=0, tiled=True)
    samp_z, samp_norm = scaled_rows(gathered, inv_len)
    arch_z, arch_norm = scaled_rows(archive, inv_len)
    local_runs = archive.shape[0]
    block_rows = min(128, local_runs)
    block_count = local_runs // block_rows
    width = mean_coef.shape[1]
    arch_blocks = arch_z.reshape(block_count, block_rows, DIN)
    norm_blocks = arch_norm.reshape(block_count, block_rows)
    mean_blocks = mean_coef.reshape(block_count, block_rows, width)
    var_blocks = var_coef.reshape(block_count, block_rows, width)
    own_rows = samples.shape[0]

    def accumulate(totals, pieces):
        mean_sum, corr_sum = totals
        block_z, block_norm, mean_rows, var_rows = pieces
        inner_prod = lax.dot_general(
            samp_z, block_z, (((1,), (1,)), ((), ())), preferred_element_type=jnp.float32
        )
        kernel = jnp.exp(inner_prod - 0.5 * samp_norm[:, None] - 0.5 * block_norm[None, :])
        kernel_half = kernel.astype(jnp.bfloat16)
        square_half = (kernel * kernel).astype(jnp.bfloat16)
        mean_sum = mean_sum + jnp.dot(kernel_half, mean_rows, preferred_element_type=jnp.float32)
        corr_sum = corr_sum + jnp.dot(square_half, var_rows, preferred_element_type=jnp.float32)
        return ((mean_sum, corr_sum), None)

    start_pair = (
        jnp.zeros((own_rows * lax.axis_size(("wide", "grp")), width), jnp.float32),
        jnp.zeros((own_rows * lax.axis_size(("wide", "grp")), width), jnp.float32),
    )
    final_pair, unused = lax.scan(
        accumulate, start_pair, (arch_blocks, norm_blocks, mean_blocks, var_blocks)
    )
    summed = lax.psum_scatter(
        jnp.concatenate([final_pair[0], final_pair[1]], axis=1),
        ("wide", "grp"),
        scatter_dimension=0,
        tiled=True,
    )
    pred_mean = summed[:, :width]
    pred_var = 1.0 - summed[:, width:]
    return (pred_mean, pred_var)


def solution(mesh):
    in_specs = (
        P(("wide", "grp"), None),
        P(("wide", "grp"), None),
        P(),
        P(("wide", "grp"), None),
        P(("wide", "grp"), None),
    )
    out_specs = (P(("wide", "grp"), None), P(("wide", "grp"), None))
    return jax.shard_map(
        on_device, mesh=mesh, in_specs=in_specs, out_specs=out_specs, check_vma=False
    )
```

profile of v0, /device:TPU:1, one launch (start us, length us, event | category | flops | bytes accessed | tf_op | source)
XLA Modules:
  0.0 715.8 jit_solution(6088330128535756338)
XLA Ops:
  8.0 1.0 copy.11
  8.9 1.0 copy.12
  9.9 0.7 broadcast_multiply_fusion.1
  10.6 2.0 multiply_reduce_fusion.1
  12.6 199.4 %all-gather.3.cloned.1.call-done = bf16[512,4,512]{2,1,0:T(4,128)(2,1)} async-done(((bf16[1,4,512]{2,1,0:T(4,128)(2,1)}), bf16[512,4,512]{2,1,0:T(4,128)(2,1)}) %all-gather.3.cloned.1.call-update) | async-done | bytes 2097168 | tf_op jit(solution)/shard_map/all_gather | solution.py:17
  212.0 4.2 reshape.27
  216.2 2.8 multiply_reduce_fusion
  218.9 21.9 %while.13 = (s32[]{:T(128)}, f32[2048,64]{0,1:T(8,128)}, f32[2048,64]{0,1:T(8,128)}, bf16[4,128,512]{2,1,0:T(8,128)(2,1)}, bf16[2048,512]{1,0:T(8,128)(2,1)S(1)}...) while((s32[]{:T(128)}, f32[2048,64]{0,1:T(8,128)}, ...), condition=%wide.region_3.4_spmd.clone, body=%wide.region_2.3_spmd.clone.sunk | while | flops 337381504 | bytes 7563396 | solution.py:47
  219.0 1.7 fusion.28
  220.7 1.1 convolution_add_fusion.5
  221.8 1.1 convolution_add_fusion.4
  222.9 1.7 fusion.28
  224.6 2.1 convolution_add_fusion.5
  226.7 2.1 convolution_add_fusion.4
  228.9 1.7 fusion.28
  230.6 2.1 convolution_add_fusion.5
  232.7 2.1 convolution_add_fusion.4
  234.9 1.7 fusion.28
  236.6 2.1 convolution_add_fusion.5
  238.7 2.1 convolution_add_fusion.4
  240.8 1.4 copy.13
  242.2 1.4 copy.14
  243.6 1.4 pad_maximum_fusion
  245.0 462.6 %all-reduce.3.cloned.1.call-done = f32[2048,128]{1,0:T(8,128)} async-done(((f32[2048,128]{1,0:T(8,128)}), f32[2048,128]{1,0:T(8,128)}) %all-reduce.3.cloned.1.call-update) | async-done | bytes 1048592
  (16 shorter events, 2.1 us)
Async XLA Ops:
  7.2 204.8 %all-gather.3.cloned.1.call-start = ((), (), s32[]{:S(2)}) async-start(), calls=%async_computation | async-start | bytes 2101248 | tf_op jit(solution)/shard_map/all_gather | solution.py:17
  7.9 699.7 %all-reduce.3.cloned.1.call-start = ((), (), s32[]{:S(2)}) async-start(), calls=%async_computation.1 | async-start | bytes 2097152
Sparse Core Ops, SparseCore 0:
  12.6 199.3 all-gather.2
  245.1 462.4 all-reduce.2
where the time goes:
time: 717 us; the launch traced here: 716 us
  waiting for transfers between devices  663 us (92%)
  matrix products  21.8 us (3%)
  between operations  14.1 us (2%)
  local copies, waits for them, and re-layouts  9.55 us (1%)
  other arithmetic  7.5 us (1%)
    unnamed x3, waiting for transfers between devices  463 us
    all_gather x1, waiting for transfers between devices, on_device(): gathered = lax.all_gather(samples, ('wide', 'grp'), axis=0, tiled=True)  199 us
  transfers between devices with their start and end apart: 2, of which 2 were waited for; matrix products, arithmetic and copies ran while one was open for 1% of the time, Pallas kernels for 0%

commit v1 on v0

--- a/solution.py
+++ b/solution.py
@@ -14,7 +14,13 @@
 
 
 def on_device(samples, archive, inv_len, mean_coef, var_coef):
-    gathered = lax.all_gather(samples, ("wide", "grp"), axis=0, tiled=True)
+    found_now = lax.all_to_all(
+        jnp.stack(lax.axis_size(("wide", "grp")) * [samples], axis=0),
+        axis_name=("wide", "grp"),
+        split_axis=0,
+        concat_axis=0,
+    )
+    gathered = jnp.concatenate(found_now, axis=0)
     samp_z, samp_norm = scaled_rows(gathered, inv_len)
     arch_z, arch_norm = scaled_rows(archive, inv_len)
     local_runs = archive.shape[0]

time: 717 us -> 623 us (0.87)
  waiting for transfers between devices: 663 us -> 556 us
  starting transfers between devices: 0.08 us -> 24.3 us
  matrix products: 21.8 us -> 12.4 us
    all_gather x1 -> x0, waiting for transfers between devices: 199 us -> none  [on_device(): gathered = lax.all_gather(samples, ('wide', 'grp'), axis=0, tiled=True)]
    all_to_all x0 -> x1, waiting for transfers between devices: none -> 97.9 us  [on_device(): lax.all_to_all(jnp.stack(lax.axis_size(('wide', 'grp')) * [samples], axis...]
    all_to_all x0 -> x1, starting transfers between devices: none -> 24.3 us  [on_device(): lax.all_to_all(jnp.stack(lax.axis_size(('wide', 'grp')) * [samples], axis...]
    unnamed x3 -> x2, waiting for transfers between devices: 463 us -> 458 us
  transfers between devices with their start and end apart: 2 -> 2, of which waited for: 2 -> 2; matrix products, arithmetic and copies ran while one was open for 1% -> 0% of each run, Pallas kernels for 0% -> 0%
where the time goes in v1:
time: 623 us
  waiting for transfers between devices  556 us (89%)
  starting transfers between devices  24.3 us (4%)
  between operations  14.1 us (2%)
  matrix products  12.4 us (2%)
  other arithmetic  8.25 us (1%)
  local copies, waits for them, and re-layouts  7.48 us (1%)
    unnamed x2, waiting for transfers between devices  458 us
    all_to_all x1, waiting for transfers between devices, on_device(): lax.all_to_all(jnp.stack(lax.axis_size(('wide', 'grp')) * [samples], axis...  97.9 us
    all_to_all x1, starting transfers between devices, on_device(): lax.all_to_all(jnp.stack(lax.axis_size(('wide', 'grp')) * [samples], axis...  24.3 us
  transfers between devices with their start and end apart: 2, of which 2 were waited for; matrix products, arithmetic and copies ran while one was open for 0% of the time, Pallas kernels for 0%

profile of v1, /device:TPU:1, one launch (start us, length us, event | category | flops | bytes accessed | tf_op | source)
XLA Modules:
  0.0 622.7 jit_solution(14583770266473302559)
XLA Ops:
  7.2 2.6 stack.2
  9.8 24.3 %all-to-all-start = ((bf16[512,4,512]{2,1,0:T(4,128)(2,1)}), bf16[512,4,512]{2,1,0:T(4,128)(2,1)S(1)}, u32[]{:S(2)}, u32[]{:S(2)}) async-start(bf16[512,4,512]{2,1,0:T(4,128)(2,1)} %stack.2), calls=%async_computation | async-start | bytes 4194304 | tf_op jit(solution)/shard_map/all_to_all | solution.py:17
  34.3 0.8 copy.16
  35.1 2.0 multiply_reduce_fusion.1
  37.1 97.9 %all-to-all-done = bf16[512,4,512]{2,1,0:T(4,128)(2,1)S(1)} async-done(((bf16[512,4,512]{2,1,0:T(4,128)(2,1)}), bf16[512,4,512]{2,1,0:T(4,128)(2,1)S(1)}, u32[]{:S(2)}, u32[]{:S(2)}) %all-to-all-start) | async-done | bytes 2097184 | tf_op jit(solution)/shard_map/all_to_all | solution.py:17
  135.0 1.4 multiply_reduce_fusion
  136.6 2.5 reshape.35
  139.1 2.8 multiply_convert_fusion.3
  141.8 12.7 %while.13 = (s32[]{:T(128)}, f32[2048,64]{0,1:T(8,128)S(1)}, f32[2048,64]{0,1:T(8,128)S(1)}, bf16[4,128,512]{2,1,0:T(8,128)(2,1)}, bf16[2048,512]{1,0:T(8,128)(2...) while((s32[]{:T(128)}, f32[2048,64]{0,1:T(8,128)S(1)}, ...), condition=%wide.region_3.4_spmd.clone, body=%wide.region_2.3_spmd.clone.sunk | while | flops 337381504 | bytes 7562896 | solution.py:53
  141.9 1.7 fusion.28
  143.6 1.1 convolution_add_fusion.5
  145.0 1.7 fusion.28
  146.8 1.1 convolution_add_fusion.5
  148.2 1.7 fusion.28
  149.9 1.1 convolution_add_fusion.5
  151.4 1.7 fusion.28
  153.1 1.1 convolution_add_fusion.5
  154.2 0.3 convolution_add_fusion.4
  154.5 0.3 copy.18
  154.8 0.3 copy.17
  155.2 1.4 pad_maximum_fusion
  156.6 457.9 %all-reduce.3.cloned.1.call-done = f32[2048,128]{1,0:T(8,128)} async-done(((f32[2048,128]{1,0:T(8,128)}), f32[2048,128]{1,0:T(8,128)}) %all-reduce.3.cloned.1.call-update) | async-done | bytes 1048592
  614.5 0.7 constant_dynamic-slice_fusion.1
  615.2 0.7 slice_subtract_fusion
  (24 shorter events, 1.3 us)
Async XLA Ops:
  7.2 27.0 %copy-start = (bf16[512,64]{0,1:T(8,128)(2,1)S(1)}, bf16[512,64]{0,1:T(8,128)(2,1)}, u32[]{:S(2)}) copy-start(bf16[512,64]{0,1:T(8,128)(2,1)} %param.10) | copy-start | bytes 196612
  7.2 27.1 %copy-start.1 = (bf16[512,64]{0,1:T(8,128)(2,1)S(1)}, bf16[512,64]{0,1:T(8,128)(2,1)}, u32[]{:S(2)}) copy-start(bf16[512,64]{0,1:T(8,128)(2,1)} %param.11) | copy-start | bytes 196612
  7.2 27.9 %copy-start.2 = (f32[512]{0:T(512)S(1)}, f32[512]{0:T(512)}, u32[]{:S(2)}) copy-start(f32[512]{0:T(512)} %param.9) | copy-start | bytes 6148
  9.8 125.2 %all-to-all-start = ((bf16[512,4,512]{2,1,0:T(4,128)(2,1)}), bf16[512,4,512]{2,1,0:T(4,128)(2,1)S(1)}, u32[]{:S(2)}, u32[]{:S(2)}) async-start(bf16[512,4,512]{2,1,0:T(4,128)(2,1)} %stack.2), calls=%async_computation | async-start | bytes 4194304 | tf_op jit(solution)/shard_map/all_to_all | solution.py:17
  34.1 580.4 %all-reduce.3.cloned.1.call-start = ((), (), s32[]{:S(2)}) async-start(), calls=%async_computation.1 | async-start | bytes 2097152
Sparse Core Ops, SparseCore 0:
  156.7 457.7 all-reduce.2
